TPU v7x, 32 devices: a whole 2x2x4 slice. The times are simulated.
32 devices in a mesh: seq: 8 (over y, x, core), mp: 4 (over z).
Axes of the slice: x: 2, y: 2, z: 4, core: 2. Of those that a mesh axis runs over, the one named last changes fastest.
Arguments:
- stream: float32 [4096, 2048], P('seq', 'mp'), may hold values from -6 to 6
- doc_starts: int32 [4096], P('seq'), may hold values 0 or 1
- gain_first: float32 [2048], replicated, may hold values from 0.5 to 1.5
- proj_inner: bfloat16 [2048, 2560], P(None, 'mp'), may hold values from -0.125 to 0.125
- proj_gate: bfloat16 [2048, 2560], P(None, 'mp'), may hold values from -0.125 to 0.125
- conv_weight: float32 [4, 2560], P(None, 'mp'), may hold values from -3 to 3
- conv_bias: float32 [2560], P('mp'), may hold values from -3 to 3
- gate_recur: bfloat16 [16, 160, 160], P('mp'), may hold values from -0.5 to 0.5
- gate_input: bfloat16 [16, 160, 160], P('mp'), may hold values from -0.5 to 0.5
- bias_recur: float32 [2560], P('mp'), may hold values from -3 to 3
- bias_input: float32 [2560], P('mp'), may hold values from -3 to 3
- decay_param: float32 [2560], P('mp'), may hold values from 3.4 to 15, as said below
- proj_out: bfloat16 [2560, 2048], P('mp'), may hold values from -0.25 to 0.25
- gain_second: float32 [2048], replicated, may hold values from 0.5 to 1.5
- mlp_gate: bfloat16 [2048, 6144], P(None, 'mp'), may hold values from -0.125 to 0.125
- mlp_up: bfloat16 [2048, 6144], P(None, 'mp'), may hold values from -0.125 to 0.125
- mlp_down: bfloat16 [6144, 2048], P('mp'), may hold values from -0.15625 to 0.15625
- cotangent: float32 [4096, 2048], P('seq', 'mp'), may hold values from -6 to 6
Outputs:
- output: float32 [4096, 2048], P('seq', 'mp')
- grad_stream: float32 [4096, 2048], P('seq', 'mp')
- grad_gain_first: float32 [2048], replicated
- grad_proj_inner: float32 [2048, 2560], P('seq', 'mp')
- grad_proj_gate: float32 [2048, 2560], P('seq', 'mp')
- grad_conv_weight: float32 [4, 2560], P(None, 'mp')
- grad_conv_bias: float32 [2560], P('mp')
- grad_gate_recur: float32 [16, 160, 160], P('mp')
- grad_gate_input: float32 [16, 160, 160], P('mp')
- grad_bias_recur: float32 [2560], P('mp')
- grad_bias_input: float32 [2560], P('mp')
- grad_decay: float32 [2560], P('mp')
- grad_proj_out: float32 [2560, 2048], P(('mp', 'seq'))
- grad_gain_second: float32 [2048], replicated
- grad_mlp_gate: float32 [2048, 6144], P('seq', 'mp')
- grad_mlp_up: float32 [2048, 6144], P('seq', 'mp')
- grad_mlp_down: float32 [6144, 2048], P(('mp', 'seq'))
Inputs may be any that keep to these rules, and one draw needn't show every extreme that they name: decay_param is -log(exp(q) - 1) for a per-channel rate q between 0.05 / 4096 and 0.03. `doc_starts`: a 1 marks the first token of a document.
All inputs are finite; a program needn't handle non-finite values. No bound on the sum of `doc_starts` on one device may be relied on, other than what follows from the above.
Results may differ from a plain program's by a relative error of at most 0.0089.
Values sent between devices are 32-bit elements; how exact they have to be, the bound alone decides.
No kernel may reach another device: no remote copies, remote signals or barrier semaphores. Data moves between devices by JAX's collectives and lax.ppermute only.
A program may use at most 256 MiB of HBM per device.

v0:
```python
from functools import partial
import jax
import jax.numpy as jnp
from jax import lax
from jax.sharding import PartitionSpec as P

recur_scale = 8.0
norm_eps = 1e-06


def passed_along(value, axis, steps):
    count = lax.axis_size(axis)
    first, last = (max(0, -steps), min(count, count - steps))
    return lax.ppermute(value, axis, [(source, source + steps) for source in range(first, last)])


def carried_in(value, axis, join, neutral, backward):
    count, mine = (lax.axis_size(axis), lax.axis_index(axis))
    pieces = jax.tree.map(lambda part: lax.all_gather(part, axis), value)
    if backward:
        pieces = jax.tree.map(lambda part: part[::-1], pieces)
        mine = count - 1 - mine
    running = jax.tree.map(
        lambda part, zero: jnp.full_like(part, 0) + jnp.asarray(zero, part.dtype), value, neutral
    )

    def turn(position, running):
        longer = join(running, jax.tree.map(lambda part: part[position], pieces))
        return jax.tree.map(lambda new, old: jnp.where(position < mine, new, old), longer, running)

    return lax.fori_loop(0, count - 1, turn, running)


def norm_rows(rows, gain):
    return rows * lax.rsqrt(jnp.mean(rows * rows, axis=-1, keepdims=True) + norm_eps) * gain


def matmul(left, right):
    return jnp.dot(left, right, preferred_element_type=jnp.float32)


def matmul_nt(left, right):
    return lax.dot_general(
        left, right, (((1,), (1,)), ((), ())), preferred_element_type=jnp.float32
    )


def matmul_tn(left, right):
    return lax.dot_general(
        left, right, (((0,), (0,)), ((), ())), preferred_element_type=jnp.float32
    )


def block_apply(values, weights):
    count = values.shape[0]
    groups = weights.shape[0]
    width = weights.shape[1]
    split = values.reshape(count, groups, width)
    mixed = jnp.einsum("tbi,bio->tbo", split, weights, preferred_element_type=jnp.float32)
    return mixed.reshape(count, groups * width)


def block_back(grads, weights):
    count = grads.shape[0]
    groups = weights.shape[0]
    width = weights.shape[1]
    split = grads.reshape(count, groups, width)
    mixed = jnp.einsum("tbo,bio->tbi", split, weights, preferred_element_type=jnp.float32)
    return mixed.reshape(count, groups * width)


def block_grad(values, grads, groups):
    count = values.shape[0]
    width = values.shape[1] // groups
    left = values.reshape(count, groups, width)
    right = grads.reshape(count, groups, width)
    return jnp.einsum("tbi,tbo->bio", left, right, preferred_element_type=jnp.float32)


def link(earlier, later):
    return (later[0] * earlier[0], later[0] * earlier[1] + later[1])


def local_scan(starts, conv_out, recur_pre, input_pre, decay):
    recur = jax.nn.sigmoid(recur_pre)
    entry = jax.nn.sigmoid(input_pre)
    log_decay = -recur_scale * recur * jax.nn.softplus(-decay)
    factor = starts + (1.0 - starts) * jnp.sqrt(-jnp.expm1(2.0 * log_decay))
    carry = jnp.exp(log_decay) * (1.0 - starts)
    fresh = factor * entry * conv_out
    return lax.associative_scan(link, (carry, fresh), axis=0)


def body(
    stream,
    doc_starts,
    gain_first,
    proj_inner,
    proj_gate,
    conv_weight,
    conv_bias,
    gate_recur,
    gate_input,
    bias_recur,
    bias_input,
    decay_param,
    proj_out,
    gain_second,
    mlp_gate,
    mlp_up,
    mlp_down,
    cotangent,
):
    count = stream.shape[0]
    own_width = stream.shape[1]
    inner_width = proj_inner.shape[1]
    ffn_width = mlp_gate.shape[1]
    groups = gate_recur.shape[0]
    lag = conv_weight.shape[0] - 1
    column = lax.axis_index("mp") * own_width
    rows_full = lax.all_gather(stream, "mp", axis=1, tiled=True)
    first_norm, first_back = jax.vjp(norm_rows, rows_full, gain_first)
    first_low = first_norm.astype(jnp.bfloat16)
    inner = matmul(first_low, proj_inner)
    gate_pre = matmul(first_low, proj_gate)
    starts = doc_starts.astype(jnp.float32)[:, None]
    keep = 1.0 - starts
    tail_keep = jnp.concatenate([keep[count - lag + 1 :], jnp.ones((1, 1), jnp.float32)], 0)
    tail_mask = jnp.flip(jnp.cumprod(jnp.flip(tail_keep, 0), 0), 0)
    prior = passed_along(inner[count - lag :] * tail_mask, "seq", 1)
    ext_inner = jnp.concatenate([prior, inner], 0)
    ext_keep = jnp.concatenate([jnp.ones((lag, 1), jnp.float32), keep], 0)
    valid = jnp.ones((count, 1), jnp.float32)
    valids = []
    conv_out = conv_weight[0] * inner
    for k in range(1, lag + 1):
        valid = valid * ext_keep[lag - k + 1 : lag - k + 1 + count]
        valids.append(valid)
        conv_out = conv_out + conv_weight[k] * ext_inner[lag - k : lag - k + count] * valid
    conv_out = conv_out + conv_bias
    conv_low = conv_out.astype(jnp.bfloat16)
    recur_pre = block_apply(conv_low, gate_recur) + bias_recur
    input_pre = block_apply(conv_low, gate_input) + bias_input
    scan_fn = partial(local_scan, starts)
    (span, partial_state), scan_back = jax.vjp(scan_fn, conv_out, recur_pre, input_pre, decay_param)
    identity = (jnp.ones((inner_width,), jnp.float32), jnp.zeros((inner_width,), jnp.float32))
    entering = carried_in(
        (span[count - 1], partial_state[count - 1]), "seq", link, identity, False
    )[1]
    states = span * entering + partial_state
    gated, gelu_back = jax.vjp(jax.nn.gelu, gate_pre)
    mixed_low = (gated * states).astype(jnp.bfloat16)
    branch = lax.psum(matmul(mixed_low, proj_out), "mp")
    resid = rows_full + branch
    second_norm, second_back = jax.vjp(norm_rows, resid, gain_second)
    second_low = second_norm.astype(jnp.bfloat16)
    ffn_gate = matmul(second_low, mlp_gate)
    ffn_up = matmul(second_low, mlp_up)
    ffn_act, act_back = jax.vjp(jax.nn.gelu, ffn_gate)
    hidden_low = (ffn_act * ffn_up).astype(jnp.bfloat16)
    mlp_own = lax.psum_scatter(matmul(hidden_low, mlp_down), "mp", scatter_dimension=1, tiled=True)
    output = lax.dynamic_slice_in_dim(resid, column, own_width, 1) + mlp_own
    cot_full = lax.all_gather(cotangent, "mp", axis=1, tiled=True)
    cot_low = cot_full.astype(jnp.bfloat16)
    d_hidden = matmul_nt(cot_low, mlp_down)
    d_gate_ffn = act_back(d_hidden * ffn_up)[0]
    d_pair_low = jnp.concatenate([d_gate_ffn, d_hidden * ffn_act], 1).astype(jnp.bfloat16)
    d_second_part = matmul_nt(d_pair_low[:, :ffn_width], mlp_gate) + matmul_nt(
        d_pair_low[:, ffn_width:], mlp_up
    )
    d_second = lax.psum(d_second_part, "mp")
    d_resid_norm, d_gain_second = second_back(d_second)
    d_resid = cot_full + d_resid_norm
    branch_low = d_resid.astype(jnp.bfloat16)
    d_mixed = matmul_nt(branch_low, proj_out)
    d_states = d_mixed * gated
    d_gate_low = gelu_back(d_mixed * states)[0].astype(jnp.bfloat16)
    outgoing = jnp.sum(d_states * span, axis=0)
    incoming = carried_in((span[count - 1], outgoing), "seq", link, identity, True)[1]
    d_total = d_states.at[count - 1].add(incoming)
    d_conv_direct, d_recur, d_input, d_decay = scan_back((d_total * entering, d_total))
    d_recur_low = d_recur.astype(jnp.bfloat16)
    d_input_low = d_input.astype(jnp.bfloat16)
    d_conv = (
        d_conv_direct + block_back(d_recur_low, gate_recur) + block_back(d_input_low, gate_input)
    )
    grad_gate_recur = block_grad(conv_low, d_recur_low, groups)
    grad_gate_input = block_grad(conv_low, d_input_low, groups)
    grad_bias_recur = jnp.sum(d_recur_low.astype(jnp.float32), axis=0)
    grad_bias_input = jnp.sum(d_input_low.astype(jnp.float32), axis=0)
    ext_grad = (
        jnp.zeros((count + lag, inner_width), jnp.float32).at[lag:].add(conv_weight[0] * d_conv)
    )
    conv_terms = [jnp.sum(d_conv * inner, axis=0)]
    for k in range(1, lag + 1):
        weighted = d_conv * valids[k - 1]
        ext_grad = ext_grad.at[lag - k : lag - k + count].add(conv_weight[k] * weighted)
        conv_terms.append(jnp.sum(weighted * ext_inner[lag - k : lag - k + count], axis=0))
    grad_conv_weight = jnp.stack(conv_terms, 0)
    grad_conv_bias = jnp.sum(d_conv, axis=0)
    returned = passed_along(ext_grad[:lag], "seq", -1)
    d_inner = ext_grad[lag:].at[count - lag :].add(returned * tail_mask)
    d_inner_low = d_inner.astype(jnp.bfloat16)
    first_pair_low = jnp.concatenate([d_inner_low, d_gate_low], 1)
    d_first_part = matmul_nt(d_inner_low, proj_inner) + matmul_nt(d_gate_low, proj_gate)
    d_first = lax.psum(d_first_part, "mp")
    d_rows_norm, d_gain_first = first_back(d_first)
    grad_stream = lax.dynamic_slice_in_dim(d_resid + d_rows_norm, column, own_width, 1)
    small = lax.psum(
        (
            d_gain_first,
            d_gain_second,
            grad_conv_weight,
            grad_conv_bias,
            grad_gate_recur,
            grad_gate_input,
            grad_bias_recur,
            grad_bias_input,
            d_decay,
        ),
        "seq",
    )
    grad_first, grad_out, grad_pair, grad_down = (
        lax.psum_scatter(
            matmul_tn(first_low, first_pair_low), "seq", scatter_dimension=0, tiled=True
        ),
        lax.psum_scatter(matmul_tn(mixed_low, branch_low), "seq", scatter_dimension=0, tiled=True),
        lax.psum_scatter(matmul_tn(second_low, d_pair_low), "seq", scatter_dimension=0, tiled=True),
        lax.psum_scatter(matmul_tn(hidden_low, cot_low), "seq", scatter_dimension=0, tiled=True),
    )
    return (
        output,
        grad_stream,
        small[0],
        grad_first[:, :inner_width],
        grad_first[:, inner_width:],
        small[2],
        small[3],
        small[4],
        small[5],
        small[6],
        small[7],
        small[8],
        grad_out,
        small[1],
        grad_pair[:, :ffn_width],
        grad_pair[:, ffn_width:],
        grad_down,
    )


def solution(mesh):
    in_specs = (
        P("seq", "mp"),
        P("seq"),
        P(),
        P(None, "mp"),
        P(None, "mp"),
        P(None, "mp"),
        P("mp"),
        P("mp", None, None),
        P("mp", None, None),
        P("mp"),
        P("mp"),
        P("mp"),
        P("mp", None),
        P(),
        P(None, "mp"),
        P(None, "mp"),
        P("mp", None),
        P("seq", "mp"),
    )
    out_specs = (
        P("seq", "mp"),
        P("seq", "mp"),
        P(),
        P("seq", "mp"),
        P("seq", "mp"),
        P(None, "mp"),
        P("mp"),
        P("mp", None, None),
        P("mp", None, None),
        P("mp"),
        P("mp"),
        P("mp"),
        P(("mp", "seq"), None),
        P(),
        P("seq", "mp"),
        P("seq", "mp"),
        P(("mp", "seq"), None),
    )
    return jax.shard_map(body, mesh=mesh, in_specs=in_specs, out_specs=out_specs, check_vma=False)
```

profile of v0, /device:TPU:0, one launch (start us, length us, event | category | flops | bytes accessed | tf_op | source)
XLA Modules:
  0.0 1586.7 jit_solution(3280703168751612168)
XLA Ops:
  10.0 83.1 %all-gather.7.cloned.1.call-done = f32[512,2048]{1,0:T(8,128)} async-done(((f32[512,512]{1,0:T(8,128)}), f32[512,2048]{1,0:T(8,128)}) %all-gather.7.cloned.1.call-update) | async-done | bytes 4194320 | tf_op jit(solution)/shard_map/all_gather | solution.py:121
  103.9 5.4 fusion.68
  121.4 4.7 exponential_multiply_fusion
  130.3 4.5 slice.593
  134.8 4.3 slice.592
  144.1 4.3 slice.675
  219.0 4.8 pad.543
  226.0 4.8 pad.561
  234.6 4.8 pad.560
  240.2 12.3 all-gather.2
  255.1 4.8 pad.542
  260.7 8.2 all-gather.1
  269.5 5.7 while.34
  275.2 7.2 multiply_convert_fusion.4
  287.9 152.0 %all-reduce.129.cloned.1.call-done = f32[512,2048]{1,0:T(8,128)} async-done(((f32[512,2048]{1,0:T(8,128)}), f32[512,2048]{1,0:T(8,128)}) %all-reduce.129.cloned.1.call-update) | async-done | bytes 4194320 | tf_op jit(solution)/shard_map/psum | solution.py:153
  446.0 10.0 fusion.115
  456.0 5.1 fusion.114
  461.1 60.2 %all-gather.9.cloned.1.call-done = f32[512,2048]{1,0:T(8,128)} async-done(((f32[512,512]{1,0:T(8,128)}), f32[512,2048]{1,0:T(8,128)}) %all-gather.9.cloned.1.call-update) | async-done | bytes 4194320 | tf_op jit(solution)/shard_map/all_gather | solution.py:163
  521.3 12.5 multiply_convert_fusion.2
  533.8 6.7 fusion.117
  540.6 7.9 convolution_add_fusion.1
  551.2 9.5 fusion.116
  560.8 141.4 %all-reduce.131.cloned.1.call-done = f32[512,2048]{1,0:T(8,128)} async-done(((f32[512,2048]{1,0:T(8,128)}), f32[512,2048]{1,0:T(8,128)}) %all-reduce.131.cloned.1.call-update) | async-done | bytes 4194320 | tf_op jit(solution)/shard_map/psum | solution.py:171
  702.2 5.2 multiply_reduce_fusion
  712.3 7.2 multiply_reduce_fusion.11
  719.5 9.0 all-gather.3
  732.1 5.7 while.35
  759.8 4.3 slice.681
  876.4 4.9 pad.680
  886.7 5.1 pad.621
  891.7 4.9 pad.681
  899.8 5.8 multiply_reduce_fusion.6
  922.2 6.3 multiply_reduce_fusion.9
  931.5 4.4 scatter-add.24
  938.9 4.4 scatter-add.25
  952.4 6.8 convolution_add_fusion
  959.3 8.6 fusion.25
  968.0 14.3 fusion.8
  988.0 6.0 fusion.30
  994.1 10.6 fusion.34
  1007.6 106.2 %all-reduce.133.cloned.1.call-done = f32[512,2048]{1,0:T(8,128)} async-done(((f32[512,2048]{1,0:T(8,128)}), f32[512,2048]{1,0:T(8,128)}) %all-reduce.133.cloned.1.call-update) | async-done | bytes 4194320 | tf_op jit(solution)/shard_map/psum | solution.py:206
  1113.8 6.4 multiply_reduce_fusion.1
  1120.2 25.1 %all-reduce.122 = (f32[2048]{0:T(1024)}, f32[4,640]{1,0:T(4,128)}, f32[640]{0:T(1024)}, f32[640]{0:T(1024)}, f32[640]{0:T(1024)}, /*index=5*/f32[640]{0:T(1024)}, f32[2048]{0:T(1024)}) all-reduce(f32[2048]{0:T(1024)S(1)} %get-tuple-element.317, f32[4,640]{1,0:T(4,128)S(1)} %pad_maximum_fusion.15, ...), channel_id=1, replica_groups=mesh['seq'=8,'mp'=4] {'seq'}, use_global_device_ids=true, to_apply=%region_15.16 | all-reduce | flops 9216 | bytes 73728 | tf_op jit(solution)/shard_map/psum | solution.py:209
  1148.4 49.5 %reduce-scatter.8.cloned.1.call-done = f32[256,1280]{1,0:T(8,128)} async-done(((f32[2048,1280]{1,0:T(8,128)}), f32[256,1280]{1,0:T(8,128)}) %reduce-scatter.8.cloned.1.call-update) | async-done | bytes 1310736 | tf_op jit(solution)/shard_map/reduce_scatter | solution.py:224
  1200.3 158.1 %reduce-scatter.12.cloned.1.call-done = f32[256,3072]{1,0:T(8,128)} async-done(((f32[2048,3072]{1,0:T(8,128)}), f32[256,3072]{1,0:T(8,128)}) %reduce-scatter.12.cloned.1.call-update) | async-done | bytes 3145744 | tf_op jit(solution)/shard_map/reduce_scatter | solution.py:228
  1362.1 58.5 %all-reduce.135.cloned.1.call-done = (f32[4,160,160]{2,1,0:T(8,128)}, f32[4,160,160]{2,1,0:T(8,128)}) async-done(((f32[4,160,160]{2,1,0:T(8,128)}, f32[4,160,160]{2,1,0:T(8,128)}), (f32[4,160,160]{2,1,0:T(8,128)}, f32[4,160,160]{2,1,0:T(8,128)})) %all-reduce.135.cloned.1.call-update) | async-done | bytes 819216 | tf_op jit(solution)/shard_map/psum | solution.py:209
  1420.6 60.0 %reduce-scatter.10.cloned.1.call-done = f32[80,2048]{1,0:T(8,128)} async-done(((f32[640,2048]{1,0:T(8,128)}), f32[80,2048]{1,0:T(8,128)}) %reduce-scatter.10.cloned.1.call-update) | async-done | bytes 655376 | tf_op jit(solution)/shard_map/reduce_scatter | solution.py:227
  1480.6 96.5 %reduce-scatter.14.cloned.1.call-done = f32[192,2048]{1,0:T(8,128)} async-done(((f32[1536,2048]{1,0:T(8,128)}), f32[192,2048]{1,0:T(8,128)}) %reduce-scatter.14.cloned.1.call-update) | async-done | bytes 1572880 | tf_op jit(solution)/shard_map/reduce_scatter | solution.py:229
  (794 shorter events, 342.8 us)
Async XLA Ops:
  7.2 268.0 %copy-start = (bf16[2048,640]{1,0:T(8,128)(2,1)S(1)}, bf16[2048,640]{1,0:T(8,128)(2,1)}, u32[]{:S(2)}) copy-start(bf16[2048,640]{1,0:T(8,128)(2,1)} %param.38) | copy-start | bytes 7864324
  7.2 85.9 %all-gather.7.cloned.1.call-start = ((), (), s32[]{:S(2)}) async-start(), calls=%async_computation.5 | async-start | bytes 5242880 | tf_op jit(solution)/shard_map/all_gather | solution.py:121
  7.9 431.9 %all-reduce.129.cloned.1.call-start = ((), (), s32[]{:S(2)}) async-start(), calls=%async_computation.6 | async-start | bytes 8388608 | tf_op jit(solution)/shard_map/psum | solution.py:153
  8.7 112.7 %copy-start.115 = (f32[512]{0:T(512)}, f32[512]{0:T(512)S(1)}, u32[]{:S(2)}) copy-start(f32[512]{0:T(512)S(1)} %broadcast_subtract_fusion) | copy-start | bytes 6148
  9.2 90.9 %copy-start.180 = (f32[3,1]{0,1:T(1,128)}, f32[3,1]{0,1:T(1,128)S(1)}, u32[]{:S(2)}) copy-start(f32[3,1]{0,1:T(1,128)S(1)} %rev.14) | copy-start | bytes 40
  9.3 94.6 %copy-start.160 = (f32[512,1]{0,1:T(1,128)}, f32[512,1]{0,1:T(1,128)S(1)}, u32[]{:S(2)}) copy-start(f32[512,1]{0,1:T(1,128)S(1)} %get-tuple-element.399) | copy-start | bytes 6148
  9.3 94.6 %copy-start.162 = (f32[512,1]{0,1:T(1,128)}, f32[512,1]{0,1:T(1,128)S(1)}, u32[]{:S(2)}) copy-start(f32[512,1]{0,1:T(1,128)S(1)} %get-tuple-element.400) | copy-start | bytes 6148
  9.3 86.5 %copy-start.164 = (f32[2048]{0:T(1024)S(1)}, f32[2048]{0:T(1024)}, u32[]{:S(2)}) copy-start(f32[2048]{0:T(1024)} %param.36) | copy-start | bytes 24580
  10.0 111.4 %copy-start.117 = (f32[640]{0:T(1024)}, f32[640]{0:T(1024)S(1)}, u32[]{:S(2)}) copy-start(f32[640]{0:T(1024)S(1)} %broadcast_multiply_fusion.3) | copy-start | bytes 7684
  101.3 2.6 collective-permute-start
  103.6 17.7 %copy-start.166 = (f32[512]{0:T(512)}, f32[512]{0:T(512)S(1)}, u32[]{:S(2)}) copy-start(f32[512]{0:T(512)S(1)} %convert_element_type.44) | copy-start | bytes 6148
  130.3 22.3 %copy-start.17 = (f32[256,640]{1,0:T(8,128)}, f32[256,640]{1,0:T(8,128)S(1)}, u32[]{:S(2)}) copy-start(f32[256,640]{1,0:T(8,128)S(1)} %slice.594) | copy-start | bytes 1966084
  155.0 9.3 copy-start.28
  189.9 9.7 copy-start.22
  287.1 234.3 %all-gather.9.cloned.1.call-start = ((), (), s32[]{:S(2)}) async-start(), calls=%async_computation.8 | async-start | bytes 5242880 | tf_op jit(solution)/shard_map/all_gather | solution.py:163
  287.8 156.1 %copy-start.129 = (f32[2048]{0:T(1024)S(1)}, f32[2048]{0:T(1024)}, u32[]{:S(2)}) copy-start(f32[2048]{0:T(1024)} %param.47) | copy-start | bytes 24580
  287.8 414.3 %all-reduce.131.cloned.1.call-start = ((), (), s32[]{:S(2)}) async-start(), calls=%async_computation.9 | async-start | bytes 8388608 | tf_op jit(solution)/shard_map/psum | solution.py:171
  443.9 12.1 slice-start.14
  446.0 10.0 copy-start.46
  446.0 10.0 slice-start.15
  548.5 456.3 %reduce-scatter.6.cloned.1.call-start = ((), (), s32[]{:S(2)}) async-start(), calls=%async_computation.7 | async-start | bytes 5242880 | tf_op jit(solution)/shard_map/reduce_scatter | solution.py:161
  560.7 141.5 %copy-start.170 = (f32[512]{0:T(512)S(1)}, f32[512]{0:T(512)}, u32[]{:S(2)}) copy-start(f32[512]{0:T(512)} %copy-done.169) | copy-start | bytes 6148
  560.7 553.0 %all-reduce.133.cloned.1.call-start = ((), (), s32[]{:S(2)}) async-start(), calls=%async_computation.10 | async-start | bytes 8388608 | tf_op jit(solution)/shard_map/psum | solution.py:206
  803.3 14.4 copy-start.36
  804.9 11.1 copy-start.114
  807.5 10.2 copy-start.119
  808.4 9.4 copy-start.120
  827.1 11.4 copy-start.64
  829.7 12.3 copy-start.92
  831.0 12.4 copy-start.49
  831.0 12.4 copy-start.51
  831.0 12.4 slice-start.6
  831.0 12.4 slice-start.7
  845.5 9.5 copy-start.70
  847.0 9.5 copy-start.33
  847.0 9.5 slice-start.4
  847.0 9.5 slice-start.5
  946.4 5.3 collective-permute-start.1
  959.3 238.6 %reduce-scatter.8.cloned.1.call-start = ((), (), s32[]{:S(2)}) async-start(), calls=%async_computation.11 | async-start | bytes 11796480 | tf_op jit(solution)/shard_map/reduce_scatter | solution.py:224
  967.9 390.5 %reduce-scatter.12.cloned.1.call-start = ((), (), s32[]{:S(2)}) async-start(), calls=%async_computation.13 | async-start | bytes 28311552 | tf_op jit(solution)/shard_map/reduce_scatter | solution.py:228
  982.3 438.3 %all-reduce.135.cloned.1.call-start = ((), (), s32[]{:S(2)}) async-start(), calls=%async_computation.15 | async-start | bytes 2621440 | tf_op jit(solution)/shard_map/psum | solution.py:209
  986.9 493.7 %reduce-scatter.10.cloned.1.call-start = ((), (), s32[]{:S(2)}) async-start(), calls=%async_computation.12 | async-start | bytes 5898240 | tf_op jit(solution)/shard_map/reduce_scatter | solution.py:227
  994.1 583.0 %reduce-scatter.14.cloned.1.call-start = ((), (), s32[]{:S(2)}) async-start(), calls=%async_computation.14 | async-start | bytes 14155776 | tf_op jit(solution)/shard_map/reduce_scatter | solution.py:229
  1004.8 108.9 %copy-start.159 = (f32[512]{0:T(512)S(1)}, f32[512]{0:T(512)}, u32[]{:S(2)}) copy-start(f32[512]{0:T(512)} %copy-done.158) | copy-start | bytes 6148
  1004.8 108.9 %copy-start.165 = (f32[2048]{0:T(1024)S(1)}, f32[2048]{0:T(1024)}, u32[]{:S(2)}) copy-start(f32[2048]{0:T(1024)} %param.36) | copy-start | bytes 24580
  1007.6 112.6 %copy-start.168 = (f32[2048]{0:T(1024)S(1)}, f32[2048]{0:T(1024)}, u32[]{:S(2)}) copy-start(f32[2048]{0:T(1024)} %get-tuple-element.315) | copy-start | bytes 24580
  1007.6 137.7 %copy-start.173 = (f32[512]{0:T(512)S(1)}, f32[512]{0:T(512)}, u32[]{:S(2)}) copy-start(f32[512]{0:T(512)} %copy-done.172) | copy-start | bytes 6148
  1420.6 158.5 %copy-start.72 = (f32[4,160,160]{2,1,0:T(8,128)S(1)}, f32[4,160,160]{2,1,0:T(8,128)}, u32[]{:S(2)}) copy-start(f32[4,160,160]{2,1,0:T(8,128)} %get-tuple-element.666) | copy-start | bytes 1228804
  (167 other events, 666.6 us)
Sparse Core Ops, SparseCore 0:
  9.6 83.4 all-gather.6
  287.2 152.6 all-reduce.128
  441.5 79.7 all-gather.8
  548.6 153.4 all-reduce.130
  704.3 75.7 reduce-scatter.5
  959.4 154.2 all-reduce.132
  1117.2 80.5 reduce-scatter.7
  1201.5 156.8 reduce-scatter.11
  1362.8 57.8 all-reduce.134
  1424.8 55.7 reduce-scatter.9
  1484.7 92.3 reduce-scatter.13
where the time goes:
time: 1600 us; the launch traced here: 1590 us
  waiting for transfers between devices  967 us (60%)
  local copies, waits for them, and re-layouts  262 us (16%)
  other arithmetic  146 us (9%)
  matrix products  136 us (8%)
  blocking collectives  54.6 us (3%)
  between operations  16.9 us (1%)
    reduce_scatter x1, waiting for transfers between devices, body(): lax.psum_scatter(matmul_tn(second_low, d_pair_low), 'seq', scatter_dimens...  158 us
    psum x1, waiting for transfers between devices, body(): branch = lax.psum(matmul(mixed_low, proj_out), 'mp')  152 us
    psum x1, waiting for transfers between devices, body(): d_second = lax.psum(d_second_part, 'mp')  141 us
    pad x94, local copies, waits for them, and re-layouts, local_scan(): return lax.associative_scan(link, (carry, fresh), axis=0)  112 us
    psum x1, waiting for transfers between devices, body(): d_first = lax.psum(d_first_part, 'mp')  106 us
    reduce_scatter x1, waiting for transfers between devices, body(): lax.psum_scatter(matmul_tn(hidden_low, cot_low), 'seq', scatter_dimension...  96.5 us
    all_gather x1, waiting for transfers between devices, body(): rows_full = lax.all_gather(stream, 'mp', axis=1, tiled=True)  83.1 us
    slice x92, local copies, waits for them, and re-layouts, local_scan(): return lax.associative_scan(link, (carry, fresh), axis=0)  81.5 us
  transfers between devices with their start and end apart: 13, of which 11 were waited for; matrix products, arithmetic and copies ran while one was open for 21% of the time, Pallas kernels for 0%

commit v1 on v0

--- a/solution.py
+++ b/solution.py
@@ -203,7 +203,8 @@
     d_inner_low = d_inner.astype(jnp.bfloat16)
     first_pair_low = jnp.concatenate([d_inner_low, d_gate_low], 1)
     d_first_part = matmul_nt(d_inner_low, proj_inner) + matmul_nt(d_gate_low, proj_gate)
-    d_first = lax.psum(d_first_part, "mp")
+    parts = lax.all_gather(d_first_part, "mp")
+    d_first = jnp.sum(parts, axis=0)
     d_rows_norm, d_gain_first = first_back(d_first)
     grad_stream = lax.dynamic_slice_in_dim(d_resid + d_rows_norm, column, own_width, 1)
     small = lax.psum(

time: 1600 us -> 1730 us (1.081)
  waiting for transfers between devices: 967 us -> 1080 us
    all_gather x0 -> x1, waiting for transfers between devices: none -> 286 us  [body(): parts = lax.all_gather(d_first_part, 'mp')]
    psum x1 -> x0, waiting for transfers between devices: 106 us -> none  [body(): d_first = lax.psum(d_first_part, 'mp')]
    reduce_scatter x1, waiting for transfers between devices: 158 us -> 111 us  [body(): lax.psum_scatter(matmul_tn(second_low, d_pair_low), 'seq', scatter_dimens...]
  transfers between devices with their start and end apart: 13 -> 13, of which waited for: 11 -> 12; matrix products, arithmetic and copies ran while one was open for 21% -> 21% of each run, Pallas kernels for 0% -> 0%
where the time goes in v1:
time: 1730 us; the launch traced here: 1720 us
  waiting for transfers between devices  1080 us (62%)
  local copies, waits for them, and re-layouts  263 us (15%)
  other arithmetic  160 us (9%)
  matrix products  134 us (8%)
  blocking collectives  55.1 us (3%)
    all_gather x1, waiting for transfers between devices, body(): parts = lax.all_gather(d_first_part, 'mp')  286 us
    psum x1, waiting for transfers between devices, body(): branch = lax.psum(matmul(mixed_low, proj_out), 'mp')  152 us
    psum x1, waiting for transfers between devices, body(): d_second = lax.psum(d_second_part, 'mp')  141 us
    pad x94, local copies, waits for them, and re-layouts, local_scan(): return lax.associative_scan(link, (carry, fresh), axis=0)  112 us
    reduce_scatter x1, waiting for transfers between devices, body(): lax.psum_scatter(matmul_tn(second_low, d_pair_low), 'seq', scatter_dimens...  111 us
    reduce_scatter x1, waiting for transfers between devices, body(): lax.psum_scatter(matmul_tn(hidden_low, cot_low), 'seq', scatter_dimension...  96.9 us
    all_gather x1, waiting for transfers between devices, body(): rows_full = lax.all_gather(stream, 'mp', axis=1, tiled=True)  83.1 us
    slice x92, local copies, waits for them, and re-layouts, local_scan(): return lax.associative_scan(link, (carry, fresh), axis=0)  81.5 us
  transfers between devices with their start and end apart: 13, of which 12 were waited for; matrix products, arithmetic and copies ran while one was open for 21% of the time, Pallas kernels for 0%

profile of v1, /device:TPU:0, one launch (start us, length us, event | category | flops | bytes accessed | tf_op | source)
XLA Modules:
  0.0 1717.6 jit_solution(17833187085208074057)
XLA Ops:
  10.0 83.1 %all-gather.9.cloned.1.call-done = f32[512,2048]{1,0:T(8,128)} async-done(((f32[512,512]{1,0:T(8,128)}), f32[512,2048]{1,0:T(8,128)}) %all-gather.9.cloned.1.call-update) | async-done | bytes 4194320 | tf_op jit(solution)/shard_map/all_gather | solution.py:121
  103.9 5.4 fusion.68
  121.4 4.7 exponential_multiply_fusion
  130.3 4.5 slice.593
  134.8 4.3 slice.592
  144.1 4.3 slice.675
  219.1 4.8 pad.543
  226.1 4.8 pad.561
  234.7 4.8 pad.560
  240.3 12.3 all-gather.3
  255.2 4.9 pad.542
  260.8 8.2 all-gather.2
  269.6 5.7 while.34
  275.3 7.2 multiply_convert_fusion.4
  288.0 152.0 %all-reduce.128.cloned.1.call-done = f32[512,2048]{1,0:T(8,128)} async-done(((f32[512,2048]{1,0:T(8,128)}), f32[512,2048]{1,0:T(8,128)}) %all-reduce.128.cloned.1.call-update) | async-done | bytes 4194320 | tf_op jit(solution)/shard_map/psum | solution.py:153
  446.1 10.0 fusion.115
  456.1 5.2 fusion.114
  461.3 60.2 %all-gather.11.cloned.1.call-done = f32[512,2048]{1,0:T(8,128)} async-done(((f32[512,512]{1,0:T(8,128)}), f32[512,2048]{1,0:T(8,128)}) %all-gather.11.cloned.1.call-update) | async-done | bytes 4194320 | tf_op jit(solution)/shard_map/all_gather | solution.py:163
  521.4 12.7 multiply_convert_fusion.2
  534.2 6.7 fusion.117
  540.9 7.9 convolution_add_fusion.1
  551.6 9.5 fusion.116
  561.1 141.4 %all-reduce.130.cloned.1.call-done = f32[512,2048]{1,0:T(8,128)} async-done(((f32[512,2048]{1,0:T(8,128)}), f32[512,2048]{1,0:T(8,128)}) %all-reduce.130.cloned.1.call-update) | async-done | bytes 4194320 | tf_op jit(solution)/shard_map/psum | solution.py:171
  702.5 5.2 multiply_reduce_fusion
  712.6 7.2 multiply_reduce_fusion.11
  719.8 9.0 all-gather.4
  732.4 5.7 while.35
  760.1 4.3 slice.681
  876.8 4.9 pad.680
  887.1 5.0 pad.621
  892.1 4.9 pad.681
  900.2 5.8 multiply_reduce_fusion.6
  922.7 6.4 multiply_reduce_fusion.9
  931.9 4.4 scatter-add.24
  939.3 4.4 scatter-add.25
  950.8 8.5 fusion.25
  966.5 16.3 fusion.8
  988.4 6.1 fusion.30
  994.6 10.7 fusion.34
  1008.1 33.1 %reduce-scatter.8.cloned.1.call-done = f32[256,1280]{1,0:T(8,128)} async-done(((f32[2048,1280]{1,0:T(8,128)}), f32[256,1280]{1,0:T(8,128)}) %reduce-scatter.8.cloned.1.call-update) | async-done | bytes 1310736 | tf_op jit(solution)/shard_map/reduce_scatter | solution.py:225
  1043.6 286.0 %all-gather.13.cloned.1.call-done = f32[2048,2048]{1,0:T(8,128)} async-done(((f32[512,2048]{1,0:T(8,128)}), f32[2048,2048]{1,0:T(8,128)}) %all-gather.13.cloned.1.call-update) | async-done | bytes 16777232 | tf_op jit(solution)/shard_map/all_gather | solution.py:206
  1329.7 10.3 reduce_sum.168
  1340.0 9.0 multiply_reduce_fusion.1
  1349.0 25.6 %all-reduce.122 = (f32[2048]{0:T(1024)}, f32[4,640]{1,0:T(4,128)}, f32[640]{0:T(1024)}, f32[640]{0:T(1024)}, f32[640]{0:T(1024)}, /*index=5*/f32[640]{0:T(1024)}, f32[2048]{0:T(1024)}) all-reduce(f32[2048]{0:T(1024)S(1)} %get-tuple-element.317, f32[4,640]{1,0:T(4,128)S(1)} %pad_maximum_fusion.15, ...), channel_id=1, replica_groups=mesh['seq'=8,'mp'=4] {'seq'}, use_global_device_ids=true, to_apply=%region_15.16 | all-reduce | flops 9216 | bytes 73728 | tf_op jit(solution)/shard_map/psum | solution.py:210
  1378.0 110.8 %reduce-scatter.12.cloned.1.call-done = f32[256,3072]{1,0:T(8,128)} async-done(((f32[2048,3072]{1,0:T(8,128)}), f32[256,3072]{1,0:T(8,128)}) %reduce-scatter.12.cloned.1.call-update) | async-done | bytes 3145744 | tf_op jit(solution)/shard_map/reduce_scatter | solution.py:229
  1492.6 58.9 %all-reduce.132.cloned.1.call-done = (f32[4,160,160]{2,1,0:T(8,128)}, f32[4,160,160]{2,1,0:T(8,128)}) async-done(((f32[4,160,160]{2,1,0:T(8,128)}, f32[4,160,160]{2,1,0:T(8,128)}), (f32[4,160,160]{2,1,0:T(8,128)}, f32[4,160,160]{2,1,0:T(8,128)})) %all-reduce.132.cloned.1.call-update) | async-done | bytes 819216 | tf_op jit(solution)/shard_map/psum | solution.py:210
  1551.5 59.6 %reduce-scatter.10.cloned.1.call-done = f32[80,2048]{1,0:T(8,128)} async-done(((f32[640,2048]{1,0:T(8,128)}), f32[80,2048]{1,0:T(8,128)}) %reduce-scatter.10.cloned.1.call-update) | async-done | bytes 655376 | tf_op jit(solution)/shard_map/reduce_scatter | solution.py:228
  1611.1 96.9 %reduce-scatter.14.cloned.1.call-done = f32[192,2048]{1,0:T(8,128)} async-done(((f32[1536,2048]{1,0:T(8,128)}), f32[192,2048]{1,0:T(8,128)}) %reduce-scatter.14.cloned.1.call-update) | async-done | bytes 1572880 | tf_op jit(solution)/shard_map/reduce_scatter | solution.py:230
  (793 shorter events, 348.2 us)
Async XLA Ops:
  7.2 268.1 %copy-start = (bf16[2048,640]{1,0:T(8,128)(2,1)S(1)}, bf16[2048,640]{1,0:T(8,128)(2,1)}, u32[]{:S(2)}) copy-start(bf16[2048,640]{1,0:T(8,128)(2,1)} %param.38) | copy-start | bytes 7864324
  7.2 85.9 %all-gather.9.cloned.1.call-start = ((), (), s32[]{:S(2)}) async-start(), calls=%async_computation.5 | async-start | bytes 5242880 | tf_op jit(solution)/shard_map/all_gather | solution.py:121
  7.9 432.0 %all-reduce.128.cloned.1.call-start = ((), (), s32[]{:S(2)}) async-start(), calls=%async_computation.6 | async-start | bytes 8388608 | tf_op jit(solution)/shard_map/psum | solution.py:153
  8.7 112.7 %copy-start.115 = (f32[512]{0:T(512)}, f32[512]{0:T(512)S(1)}, u32[]{:S(2)}) copy-start(f32[512]{0:T(512)S(1)} %broadcast_subtract_fusion) | copy-start | bytes 6148
  9.2 90.9 %copy-start.180 = (f32[3,1]{0,1:T(1,128)}, f32[3,1]{0,1:T(1,128)S(1)}, u32[]{:S(2)}) copy-start(f32[3,1]{0,1:T(1,128)S(1)} %rev.14) | copy-start | bytes 40
  9.3 94.6 %copy-start.160 = (f32[512,1]{0,1:T(1,128)}, f32[512,1]{0,1:T(1,128)S(1)}, u32[]{:S(2)}) copy-start(f32[512,1]{0,1:T(1,128)S(1)} %get-tuple-element.399) | copy-start | bytes 6148
  9.3 94.6 %copy-start.162 = (f32[512,1]{0,1:T(1,128)}, f32[512,1]{0,1:T(1,128)S(1)}, u32[]{:S(2)}) copy-start(f32[512,1]{0,1:T(1,128)S(1)} %get-tuple-element.400) | copy-start | bytes 6148
  9.3 86.5 %copy-start.164 = (f32[2048]{0:T(1024)S(1)}, f32[2048]{0:T(1024)}, u32[]{:S(2)}) copy-start(f32[2048]{0:T(1024)} %param.36) | copy-start | bytes 24580
  10.0 111.4 %copy-start.117 = (f32[640]{0:T(1024)}, f32[640]{0:T(1024)S(1)}, u32[]{:S(2)}) copy-start(f32[640]{0:T(1024)S(1)} %broadcast_multiply_fusion.3) | copy-start | bytes 7684
  101.3 2.6 collective-permute-start
  103.6 17.7 %copy-start.166 = (f32[512]{0:T(512)}, f32[512]{0:T(512)S(1)}, u32[]{:S(2)}) copy-start(f32[512]{0:T(512)S(1)} %convert_element_type.44) | copy-start | bytes 6148
  130.3 22.3 %copy-start.16 = (f32[256,640]{1,0:T(8,128)}, f32[256,640]{1,0:T(8,128)S(1)}, u32[]{:S(2)}) copy-start(f32[256,640]{1,0:T(8,128)S(1)} %slice.594) | copy-start | bytes 1966084
  155.0 9.3 copy-start.27
  189.9 9.8 copy-start.21
  287.2 234.2 %all-gather.11.cloned.1.call-start = ((), (), s32[]{:S(2)}) async-start(), calls=%async_computation.8 | async-start | bytes 5242880 | tf_op jit(solution)/shard_map/all_gather | solution.py:163
  287.9 156.1 %copy-start.129 = (f32[2048]{0:T(1024)S(1)}, f32[2048]{0:T(1024)}, u32[]{:S(2)}) copy-start(f32[2048]{0:T(1024)} %param.47) | copy-start | bytes 24580
  288.0 414.6 %all-reduce.130.cloned.1.call-start = ((), (), s32[]{:S(2)}) async-start(), calls=%async_computation.9 | async-start | bytes 8388608 | tf_op jit(solution)/shard_map/psum | solution.py:171
  444.0 12.1 slice-start.14
  446.1 10.0 copy-start.46
  446.1 10.0 slice-start.15
  548.8 456.6 %reduce-scatter.6.cloned.1.call-start = ((), (), s32[]{:S(2)}) async-start(), calls=%async_computation.7 | async-start | bytes 5242880 | tf_op jit(solution)/shard_map/reduce_scatter | solution.py:161
  561.1 141.5 %copy-start.170 = (f32[512]{0:T(512)S(1)}, f32[512]{0:T(512)}, u32[]{:S(2)}) copy-start(f32[512]{0:T(512)} %copy-done.169) | copy-start | bytes 6148
  561.1 480.1 %reduce-scatter.8.cloned.1.call-start = ((), (), s32[]{:S(2)}) async-start(), calls=%async_computation.10 | async-start | bytes 11796480 | tf_op jit(solution)/shard_map/reduce_scatter | solution.py:225
  803.7 14.5 copy-start.35
  805.3 11.1 copy-start.114
  807.9 10.2 copy-start.119
  808.7 9.4 copy-start.120
  827.4 11.4 copy-start.64
  830.1 12.3 copy-start.92
  831.4 12.4 copy-start.49
  831.4 12.4 copy-start.51
  831.4 12.4 slice-start.6
  831.4 12.4 slice-start.7
  845.9 9.5 copy-start.70
  847.4 9.5 copy-start.32
  847.4 9.5 slice-start.4
  847.4 9.5 slice-start.5
  946.8 3.1 collective-permute-start.1
  959.3 370.3 %all-gather.13.cloned.1.call-start = ((), (), s32[]{:S(2)}) async-start(), calls=%async_computation.14 | async-start | bytes 20971520 | tf_op jit(solution)/shard_map/all_gather | solution.py:206
  966.4 522.4 %reduce-scatter.12.cloned.1.call-start = ((), (), s32[]{:S(2)}) async-start(), calls=%async_computation.12 | async-start | bytes 28311552 | tf_op jit(solution)/shard_map/reduce_scatter | solution.py:229
  982.8 568.7 %all-reduce.132.cloned.1.call-start = ((), (), s32[]{:S(2)}) async-start(), calls=%async_computation.15 | async-start | bytes 2621440 | tf_op jit(solution)/shard_map/psum | solution.py:210
  987.4 623.7 %reduce-scatter.10.cloned.1.call-start = ((), (), s32[]{:S(2)}) async-start(), calls=%async_computation.11 | async-start | bytes 5898240 | tf_op jit(solution)/shard_map/reduce_scatter | solution.py:228
  994.6 713.4 %reduce-scatter.14.cloned.1.call-start = ((), (), s32[]{:S(2)}) async-start(), calls=%async_computation.13 | async-start | bytes 14155776 | tf_op jit(solution)/shard_map/reduce_scatter | solution.py:230
  1329.7 10.3 copy-start.159
  1329.7 10.3 copy-start.165
  1340.0 9.0 copy-start.168
  1340.0 34.5 %copy-start.173 = (f32[512]{0:T(512)S(1)}, f32[512]{0:T(512)}, u32[]{:S(2)}) copy-start(f32[512]{0:T(512)} %copy-done.172) | copy-start | bytes 6148
  1551.5 158.5 %copy-start.72 = (f32[4,160,160]{2,1,0:T(8,128)S(1)}, f32[4,160,160]{2,1,0:T(8,128)}, u32[]{:S(2)}) copy-start(f32[4,160,160]{2,1,0:T(8,128)} %get-tuple-element.666) | copy-start | bytes 1228804
  (166 other events, 664.0 us)
Sparse Core Ops, SparseCore 0:
  9.6 83.4 all-gather.8
  287.3 152.6 all-reduce.127
  441.6 79.7 all-gather.10
  549.0 153.4 all-reduce.129
  704.6 75.7 reduce-scatter.5
  959.4 81.7 reduce-scatter.7
  1042.9 286.7 all-gather.12
  1333.7 155.0 reduce-scatter.11
  1493.5 57.9 all-reduce.131
  1555.3 55.7 reduce-scatter.9
  1615.6 92.3 reduce-scatter.13
